TPU v7x, 32 devices: a whole 2x2x4 slice. The times are simulated.
32 devices in a mesh: blk: 16 (over z, x, core), mp: 2 (over y).
Axes of the slice: x: 2, y: 2, z: 4, core: 2. Of those that a mesh axis runs over, the one named last changes fastest.
Arguments:
- features: bfloat16 [16, 2, 2, 256, 1280], P('blk', None, None, None, 'mp'), may hold values from -62 to 62
- w_query: bfloat16 [1280, 1280], P(None, 'mp'), may hold values from -2 to 2
- w_key: bfloat16 [1280, 1280], P(None, 'mp'), may hold values from -2 to 2
- w_value: bfloat16 [1280, 1280], P(None, 'mp'), may hold values from -0.15625 to 0.15625
- w_out: bfloat16 [1280, 1280], P('mp'), may hold values from -0.15625 to 0.15625
- w_head: bfloat16 [1280, 64], replicated, may hold values from -0.15625 to 0.15625
- offsets: int32 [16], P('blk'), may hold values from 0 to 255, as said below
- blend_mask: int32 [16, 64, 64], P('blk'), may hold values from 1 to 4
Outputs:
- panorama: float32 [2, 256, 256], P(None, 'blk')
Inputs may be any that keep to these rules, and one draw needn't show every extreme that they name: offsets[w] = 16 * w + s for one s shared by all windows, 0 <= s < 16.
All inputs are finite; a program needn't handle non-finite values.
Results may differ from a plain program's by a relative error of at most 0.0064.
Values may be sent and summed in bfloat16 or wider, within the bound.
No kernel may reach another device: no remote copies, remote signals or barrier semaphores. Data moves between devices by JAX's collectives and lax.ppermute only.
A program may use at most 64 MiB of HBM per device.

v0:
```python
import jax
import jax.numpy as jnp
from jax import lax
from jax.sharding import PartitionSpec as P

HEAD = 64
GRID = 16
PATCH = 4
CHAN = 4
STRIDE = 16
WINDOW = 64
OUTW = 64
guidance = 3.0


def shifted(x, axis, by):
    count = lax.axis_size(axis)
    return lax.ppermute(x, axis, [(i, (i + by) % count) for i in range(count)])


def shards(features, w_query, w_key, w_value, w_out, w_head, offsets, blend_mask):
    gathered = lax.all_gather(features, "mp", axis=4, tiled=True)
    batch_count = gathered.shape[1]
    token_count = gathered.shape[3]
    model_width = gathered.shape[4]
    sequences = batch_count * 2
    local_heads = w_query.shape[1] // HEAD
    token_plain = gathered.reshape(-1, model_width)
    token_rows = token_plain.astype(jnp.float32)
    row_mean = jnp.mean(token_rows, axis=1, keepdims=True)
    centred = token_rows - row_mean
    row_var = jnp.mean(centred * centred, axis=1, keepdims=True)
    normed = (centred * lax.rsqrt(row_var + 1e-05)).astype(jnp.bfloat16)
    queries = (
        jnp.dot(normed, w_query, preferred_element_type=jnp.float32)
        .astype(jnp.bfloat16)
        .reshape(sequences, token_count, local_heads, HEAD)
    )
    key_rows = (
        jnp.dot(normed, w_key, preferred_element_type=jnp.float32)
        .astype(jnp.bfloat16)
        .reshape(sequences, token_count, local_heads, HEAD)
    )
    value_rows = (
        jnp.dot(normed, w_value, preferred_element_type=jnp.float32)
        .astype(jnp.bfloat16)
        .reshape(sequences, token_count, local_heads, HEAD)
    )
    scores = (
        jnp.einsum("sqhd,skhd->shqk", queries, key_rows, preferred_element_type=jnp.float32)
        / HEAD**0.5
    )
    scores = scores - jnp.max(scores, axis=3, keepdims=True)
    expont = jnp.exp(scores)
    attend = (expont / jnp.sum(expont, axis=3, keepdims=True)).astype(jnp.bfloat16)
    context = jnp.einsum(
        "shqk,skhd->sqhd", attend, value_rows, preferred_element_type=jnp.float32
    ).astype(jnp.bfloat16)
    context = context.reshape(-1, local_heads * HEAD)
    partial_value = jnp.dot(context, w_out, preferred_element_type=jnp.float32)
    head_weight = w_head.astype(jnp.float32)
    head_part = jnp.dot(partial_value, head_weight, precision=lax.Precision.HIGHEST)
    tok_out = lax.psum(head_part.astype(jnp.bfloat16), "mp").astype(jnp.float32) + jnp.dot(
        token_plain, w_head, preferred_element_type=jnp.float32
    )
    tok_out = tok_out.reshape(batch_count, 2, token_count, OUTW)
    guided = tok_out[:, 0] + guidance * (tok_out[:, 1] - tok_out[:, 0])
    spread = guided.reshape(batch_count, GRID, GRID, PATCH, PATCH, CHAN).transpose(0, 2, 3, 1, 4, 5)
    spread = spread.reshape(batch_count, WINDOW, WINDOW * CHAN)
    weight = blend_mask[0].astype(jnp.float32)
    weighted = spread * jnp.repeat(weight, CHAN, axis=1)[None]
    shift_cols = offsets[0] - STRIDE * lax.axis_index("blk")
    zero_index = jnp.zeros((), jnp.int32)
    frame_num = lax.dynamic_update_slice(
        jnp.zeros((batch_count, WINDOW + STRIDE, WINDOW * CHAN), jnp.float32),
        weighted,
        (zero_index, shift_cols, zero_index),
    )
    frame_weight = lax.dynamic_update_slice(
        jnp.zeros((WINDOW + STRIDE, WINDOW), jnp.float32), weight, (shift_cols, zero_index)
    )
    piece_count = WINDOW // STRIDE + 1
    numerators = [frame_num[:, j * STRIDE : (j + 1) * STRIDE] for j in range(piece_count)]
    weight_pieces = [frame_weight[j * STRIDE : (j + 1) * STRIDE] for j in range(piece_count)]
    blended_num = numerators[0]
    blended_weight = weight_pieces[0]
    for j in range(1, piece_count):
        arrived = shifted((numerators[j], weight_pieces[j]), "blk", j)
        blended_num = blended_num + arrived[0]
        blended_weight = blended_weight + arrived[1]
    return blended_num / jnp.repeat(blended_weight, CHAN, axis=1)[None]


def solution(mesh):
    return jax.shard_map(
        shards,
        mesh=mesh,
        in_specs=(
            P("blk", None, None, None, "mp"),
            P(None, "mp"),
            P(None, "mp"),
            P(None, "mp"),
            P("mp", None),
            P(),
            P("blk"),
            P("blk", None, None),
        ),
        out_specs=P(None, "blk", None),
        check_vma=False,
    )
```

profile of v0, /device:TPU:0, one launch (start us, length us, event | category | flops | bytes accessed | tf_op | source)
XLA Modules:
  0.0 160.9 jit_solution(14204713652645674457)
XLA Ops:
  6.5 0.7 all-gather.2.cloned.1.call-update
  7.3 0.0 all-reduce.2.cloned.1.call-start
  8.0 0.8 convert_bitcast_fusion
  8.7 0.1 copy.44
  8.8 0.4 dynamic_update_slice.7
  9.3 41.4 %all-gather.2.cloned.1.call-done = bf16[1,2,2,256,1280]{4,3,2,1,0:T(8,128)(2,1)} async-done(((bf16[1,2,2,256,640]{4,3,2,1,0:T(8,128)(2,1)}), bf16[1,2,2,256,1280]{4,3,2,1,0:T(8,128)(2,1)}) %all-gather.2.cloned.1.call-update) | async-done | bytes 2621456 | tf_op jit(solution)/shard_map/all_gather | solution.py:22
  50.6 2.3 %convert_reduce_fusion = f32[2,2,256]{2,1,0:T(2,128)S(1)} fusion(bf16[1,2,2,256,1280]{4,3,2,1,0:T(8,128)(2,1)} %all-gather.2.cloned.1.call-done), kind=kLoop, calls=%fused_computation.6 | loop fusion | flops 2620416 | bytes 2625536 | tf_op jit(solution)/shard_map/reduce_sum | solution.py:30
  53.0 0.2 copy-done.1
  53.2 0.8 fusion.5
  54.0 0.0 copy-start.6
  54.0 0.7 multiply_convert_fusion
  54.7 1.5 copy-done.2
  56.2 2.2 %convolution_convert_fusion = bf16[1024,640]{1,0:T(8,128)(2,1)S(1)} fusion(bf16[1024,1280]{1,0:T(8,128)(2,1)S(1)} %multiply_convert_fusion, bf16[1280,640]{1,0:T(8,128)(2,1)S(1)} %copy-done.6), kind=kOutput, calls=%fused_computation.13 | convolution fusion | flops 1678376960 | bytes 5570560 | tf_op jit(solution)/shard_map/dot_general | solution.py:40
  58.5 1.5 copy.35
  60.0 2.9 %reshape.66 = bf16[4,256,10,64]{1,0,3,2:T(4,128)(2,1)S(1)} reshape(bf16[1024,640]{0,1:T(8,128)(2,1)} %copy.35) | data formatting | bytes 2621440 | tf_op jit(solution)/shard_map/reshape | solution.py:42
  62.9 0.0 copy-start.7
  62.9 5.6 %convolution_convert_fusion.1 = bf16[1024,640]{1,0:T(8,128)(2,1)} fusion(bf16[1024,1280]{1,0:T(8,128)(2,1)} %copy-done.2, bf16[1280,640]{1,0:T(8,128)(2,1)} %param.9), kind=kOutput, calls=%fused_computation.14 | convolution fusion | flops 1678376960 | bytes 5570560 | tf_op jit(solution)/shard_map/dot_general | solution.py:35
  68.5 3.3 %convolution_convert_fusion.2 = bf16[1024,640]{1,0:T(8,128)(2,1)} fusion(bf16[1024,1280]{1,0:T(8,128)(2,1)S(1)} %copy-done.3, bf16[1280,640]{1,0:T(8,128)(2,1)S(1)} %copy-done.7), kind=kOutput, calls=%fused_computation.15 | convolution fusion | flops 1678376960 | bytes 5570560 | tf_op jit(solution)/shard_map/dot_general | solution.py:45
  71.8 2.5 %copy.33 = bf16[1024,640]{0,1:T(8,128)(2,1)} copy(bf16[1024,640]{1,0:T(8,128)(2,1)} %convolution_convert_fusion.2) | data formatting | bytes 2621440 | tf_op jit(solution)/shard_map/convert_element_type | solution.py:46
  74.3 3.8 %reshape.64 = bf16[4,256,10,64]{1,0,3,2:T(4,128)(2,1)} reshape(bf16[1024,640]{0,1:T(8,128)(2,1)} %copy.33) | data formatting | bytes 2621440 | tf_op jit(solution)/shard_map/reshape | solution.py:47
  78.0 2.5 %copy.34 = bf16[1024,640]{0,1:T(8,128)(2,1)} copy(bf16[1024,640]{1,0:T(8,128)(2,1)} %convolution_convert_fusion.1) | data formatting | bytes 2621440 | tf_op jit(solution)/shard_map/convert_element_type | solution.py:36
  80.5 3.8 %reshape.65 = bf16[4,256,10,64]{1,0,3,2:T(4,128)(2,1)} reshape(bf16[1024,640]{0,1:T(8,128)(2,1)} %copy.34) | data formatting | bytes 2621440 | tf_op jit(solution)/shard_map/reshape | solution.py:37
  84.3 2.9 %fusion.11 = f32[4,10,256,256]{2,3,1,0:T(8,128)S(1)} fusion(bf16[4,256,10,64]{1,0,3,2:T(4,128)(2,1)S(1)} %reshape.66, bf16[4,256,10,64]{1,0,3,2:T(4,128)(2,1)} %reshape.65), kind=kOutput, calls=%fused_computation.18 | convolution fusion | flops 335544320 | bytes 13107200 | tf_op jit(solution)/shard_map/sqhd,skhd->shqk/dot_general | solution.py:50
  87.2 5.4 %fusion.23 = (f32[4,10,256]{2,1,0:T(8,128)S(1)}, f32[4,10,256,256]{2,3,1,0:T(8,128)}) fusion(f32[4,10,256,256]{2,3,1,0:T(8,128)S(1)} %fusion.11), kind=kOutput, calls=%fused_computation.39 | output fusion | flops 10486015 | bytes 21012480 | tf_op jit(solution)/shard_map/sub | solution.py:53
  92.6 4.9 %fusion.9 = bf16[4,256,10,64]{1,3,2,0:T(8,128)(2,1)S(1)} fusion(f32[4,10,256,256]{2,3,1,0:T(8,128)} %get-tuple-element.19, f32[4,10,256]{2,1,0:T(8,128)S(1)} %get-tuple-element.18, bf16[4,256,10,64]{1,0,3,2:T(4,128)(2,1)S(1)} %copy-done.4), kind=kOutput, calls=%fused_computation.16 | convolution fusion | flops 341442560 | bytes 13148160 | tf_op jit(solution)/shard_map/shqk,skhd->sqhd/dot_general | solution.py:56
  97.5 1.0 copy.40
  98.6 0.3 copy.62
  98.9 0.0 copy-start.5
  98.9 2.3 %fusion.24 = f32[1024,1280]{1,0:T(8,128)S(1)} fusion(bf16[1024,640]{0,1:T(8,128)(2,1)S(1)} %bitcast.57, bf16[640,1280]{1,0:T(8,128)(2,1)S(1)} %copy-done), kind=kOutput, calls=%fused_computation.40 | convolution fusion | flops 1677721600 | bytes 8192000 | tf_op jit(solution)/shard_map/dot_general | solution.py:60
  101.2 3.5 %convolution_convert_fusion.3 = bf16[1024,64]{0,1:T(8,128)(2,1)} fusion(f32[1024,1280]{1,0:T(8,128)S(1)} %fusion.24, bf16[1280,64]{0,1:T(8,128)(2,1)S(1)} %copy-done.5), kind=kOutput, calls=%fused_computation.22 | convolution fusion | flops 1006698496 | bytes 5537792 | tf_op jit(solution)/shard_map/dot_general | solution.py:62
  104.7 0.0 all-reduce.2.cloned.1.call-update
  104.7 0.1 fusion.22
  104.8 0.1 copy.59
  104.8 0.7 collective-permute-start.6
  105.6 0.1 copy.57
  105.6 0.9 collective-permute-start.4
  106.5 0.1 copy.58
  106.6 1.5 collective-permute-start.5
  108.0 1.5 collective-permute-start.7
  109.5 0.1 copy.56
  109.6 16.8 %all-reduce.2.cloned.1.call-done = bf16[1024,64]{0,1:T(8,128)(2,1)} async-done(((bf16[1024,64]{0,1:T(8,128)(2,1)}), bf16[1024,64]{0,1:T(8,128)(2,1)}) %all-reduce.2.cloned.1.call-update) | async-done | bytes 131088 | tf_op jit(solution)/shard_map/psum | solution.py:63
  126.3 2.6 %convolution_add_fusion = f32[1024,64]{0,1:T(8,128)S(1)} fusion(bf16[1024,1280]{1,0:T(8,128)(2,1)} %bitcast.55, bf16[1280,64]{0,1:T(8,128)(2,1)S(1)} %copy-done.5, bf16[1024,64]{0,1:T(8,128)(2,1)} %all-reduce.2.cloned.1.call-done), kind=kOutput, calls=%fused_computation.21 | convolution fusion | flops 167903232 | bytes 3178496 | tf_op jit(solution)/shard_map/dot_general | solution.py:63
  129.0 0.2 reshape.68
  129.2 0.2 fusion.20
  129.5 1.3 squeeze.11
  130.8 1.3 squeeze.12
  132.1 1.7 %add_bitcast_fusion = f32[2,16,4,16,4,4]{1,3,5,4,2,0:T(8,128)S(1)} fusion(f32[2,16,16,4,4,4]{2,1,5,4,3,0:T(8,128)} %squeeze.11, f32[2,16,16,4,4,4]{2,1,5,4,3,0:T(8,128)} %squeeze.12), kind=kLoop, calls=%fused_computation.23 | loop fusion | flops 98304 | bytes 393216 | tf_op jit(solution)/shard_map/transpose | solution.py:68
  133.8 4.7 %copy.43 = f32[2,16,4,16,4,4]{2,1,5,4,3,0:T(8,128)} copy(f32[2,16,4,16,4,4]{1,3,5,4,2,0:T(8,128)S(1)} %add_bitcast_fusion) | data formatting | bytes 262144 | tf_op jit(solution)/shard_map/transpose | solution.py:68
  138.6 3.6 %reshape.69 = f32[2,64,256]{1,2,0:T(8,128)S(1)} reshape(f32[2,16,4,16,4,4]{2,1,5,4,3,0:T(8,128)} %copy.43) | data formatting | bytes 262144 | tf_op jit(solution)/shard_map/reshape | solution.py:69
  142.3 0.1 copy.45
  142.4 0.4 dynamic_update_slice.6
  142.9 0.1 collective-permute-start
  142.9 0.0 collective-permute-done.6
  142.9 1.5 collective-permute-start.3
  144.5 0.0 collective-permute-done.4
  144.5 2.3 %collective-permute-start.2 = (f32[2,16,256]{2,1,0:T(8,128)S(1)}, f32[2,16,256]{2,1,0:T(8,128)S(1)}, u32[]{:S(2)}, u32[]{:S(2)}) collective-permute-start(f32[2,16,256]{2,1,0:T(8,128)S(1)} %get-tuple-element.9), channel_id=1, source_target_pairs={{0,6},{2,8},{4,10},{6,12},{8,14},{10,16},{12,18},{14,20},{16,22},{... | collective-permute-start | bytes 98312 | tf_op jit(solution)/shard_map/ppermute | solution.py:18
  146.8 0.0 collective-permute-done.5
  146.8 1.5 collective-permute-start.1
  148.3 0.1 copy.51
  148.4 0.1 copy.52
  148.5 0.5 collective-permute-done
  149.0 0.7 collective-permute-done.2
  149.6 3.8 %collective-permute-done.1 = f32[2,16,256]{2,1,0:T(8,128)S(1)} collective-permute-done((f32[2,16,256]{2,1,0:T(8,128)S(1)}, f32[2,16,256]{2,1,0:T(8,128)S(1)}, u32[]{:S(2)}, u32[]{:S(2)}) %collective-permute-start.1) | collective-permute-done | bytes 32800 | tf_op jit(solution)/shard_map/ppermute | solution.py:18
  153.4 0.6 fusion.17
  (28 shorter events, 0.2 us)
Async XLA Ops:
  6.5 92.3 %copy-start = (bf16[640,1280]{1,0:T(8,128)(2,1)S(1)}, bf16[640,1280]{1,0:T(8,128)(2,1)}, u32[]{:S(2)}) copy-start(bf16[640,1280]{1,0:T(8,128)(2,1)} %param.12) | copy-start | bytes 4915204
  6.5 44.1 %all-gather.2.cloned.1.call-start = ((), (), s32[]{:S(2)}) async-start(), calls=%async_computation | async-start | bytes 3932160 | tf_op jit(solution)/shard_map/all_gather | solution.py:22
  7.3 119.1 %all-reduce.2.cloned.1.call-start = ((), (), s32[]{:S(2)}) async-start(), calls=%async_computation.1 | async-start | bytes 262144 | tf_op jit(solution)/shard_map/psum | solution.py:63
  50.6 2.5 %copy-start.1 = (bf16[1,2,2,256,1280]{4,3,2,1,0:T(8,128)(2,1)S(1)}, bf16[1,2,2,256,1280]{4,3,2,1,0:T(8,128)(2,1)}, u32[]{:S(2)}) copy-start(bf16[1,2,2,256,1280]{4,3,2,1,0:T(8,128)(2,1)} %all-gather.2.cloned.1.call-done) | copy-start | bytes 7864324
  54.0 2.2 %copy-start.6 = (bf16[1280,640]{1,0:T(8,128)(2,1)S(1)}, bf16[1280,640]{1,0:T(8,128)(2,1)}, u32[]{:S(2)}) copy-start(bf16[1280,640]{1,0:T(8,128)(2,1)} %param.10) | copy-start | bytes 4915204
  54.7 1.5 copy-start.2
  62.8 5.6 %copy-start.3 = (bf16[1024,1280]{1,0:T(8,128)(2,1)S(1)}, bf16[1024,1280]{1,0:T(8,128)(2,1)}, u32[]{:S(2)}) copy-start(bf16[1024,1280]{1,0:T(8,128)(2,1)} %copy-done.2) | copy-start | bytes 7864324
  62.9 5.6 %copy-start.7 = (bf16[1280,640]{1,0:T(8,128)(2,1)S(1)}, bf16[1280,640]{1,0:T(8,128)(2,1)}, u32[]{:S(2)}) copy-start(bf16[1280,640]{1,0:T(8,128)(2,1)} %param.11) | copy-start | bytes 4915204
  87.2 5.5 %copy-start.4 = (bf16[4,256,10,64]{1,0,3,2:T(4,128)(2,1)S(1)}, bf16[4,256,10,64]{1,0,3,2:T(4,128)(2,1)}, u32[]{:S(2)}) copy-start(bf16[4,256,10,64]{1,0,3,2:T(4,128)(2,1)} %reshape.64) | copy-start | bytes 3932164
  98.9 2.3 %copy-start.5 = (bf16[1280,64]{0,1:T(8,128)(2,1)S(1)}, bf16[1280,64]{0,1:T(8,128)(2,1)}, u32[]{:S(2)}) copy-start(bf16[1280,64]{0,1:T(8,128)(2,1)} %param.13) | copy-start | bytes 491524
  104.8 38.1 %collective-permute-start.6 = (f32[16,64]{1,0:T(8,128)S(1)}, f32[16,64]{1,0:T(8,128)S(1)}, u32[]{:S(2)}, u32[]{:S(2)}) collective-permute-start(f32[16,64]{1,0:T(8,128)S(1)} %copy.59), channel_id=1, source_target_pairs={{0,6},{2,8},{4,10},{6,12},{8,14},{10,16},{12,18},{14,20},{16,22},{... | collective-permute-start | bytes 12296 | tf_op jit(solution)/shard_map/ppermute | solution.py:18
  105.6 38.8 %collective-permute-start.4 = (f32[16,64]{1,0:T(8,128)S(1)}, f32[16,64]{1,0:T(8,128)S(1)}, u32[]{:S(2)}, u32[]{:S(2)}) collective-permute-start(f32[16,64]{1,0:T(8,128)S(1)} %copy.57), channel_id=1, source_target_pairs={{0,2},{2,4},{4,6},{6,8},{8,10},{10,12},{12,14},{14,16},{16,18},{18... | collective-permute-start | bytes 12296 | tf_op jit(solution)/shard_map/ppermute | solution.py:18
  106.6 40.2 %collective-permute-start.5 = (f32[16,64]{1,0:T(8,128)S(1)}, f32[16,64]{1,0:T(8,128)S(1)}, u32[]{:S(2)}, u32[]{:S(2)}) collective-permute-start(f32[16,64]{1,0:T(8,128)S(1)} %copy.58), channel_id=1, source_target_pairs={{0,4},{2,6},{4,8},{6,10},{8,12},{10,14},{12,16},{14,18},{16,20},{1... | collective-permute-start | bytes 12296 | tf_op jit(solution)/shard_map/ppermute | solution.py:18
  108.0 40.3 %collective-permute-start.7 = (f32[16,64]{0,1:T(8,128)S(1)}, f32[16,64]{0,1:T(8,128)S(1)}, u32[]{:S(2)}, u32[]{:S(2)}) collective-permute-start(f32[16,64]{0,1:T(8,128)S(1)} %get-tuple-element.11), channel_id=1, source_target_pairs={{0,8},{2,10},{4,12},{6,14},{8,16},{10,18},{12,20},{14,22},{16,24},... | collective-permute-start | bytes 12296 | tf_op jit(solution)/shard_map/ppermute | solution.py:18
  142.9 6.1 %collective-permute-start = (f32[2,16,256]{2,1,0:T(8,128)S(1)}, f32[2,16,256]{2,1,0:T(8,128)S(1)}, u32[]{:S(2)}, u32[]{:S(2)}) collective-permute-start(f32[2,16,256]{2,1,0:T(8,128)S(1)} %get-tuple-element.7), channel_id=1, source_target_pairs={{0,2},{2,4},{4,6},{6,8},{8,10},{10,12},{12,14},{14,16},{16,18},{18... | collective-permute-start | bytes 98312 | tf_op jit(solution)/shard_map/ppermute | solution.py:18
  142.9 6.0 %collective-permute-start.3 = (f32[2,16,256]{2,1,0:T(8,128)S(1)}, f32[2,16,256]{2,1,0:T(8,128)S(1)}, u32[]{:S(2)}, u32[]{:S(2)}) collective-permute-start(f32[2,16,256]{2,1,0:T(8,128)S(1)} %get-tuple-element.8), channel_id=1, source_target_pairs={{0,8},{2,10},{4,12},{6,14},{8,16},{10,18},{12,20},{14,22},{16,24},... | collective-permute-start | bytes 98312 | tf_op jit(solution)/shard_map/ppermute | solution.py:18
  144.5 5.1 %collective-permute-start.2 = (f32[2,16,256]{2,1,0:T(8,128)S(1)}, f32[2,16,256]{2,1,0:T(8,128)S(1)}, u32[]{:S(2)}, u32[]{:S(2)}) collective-permute-start(f32[2,16,256]{2,1,0:T(8,128)S(1)} %get-tuple-element.9), channel_id=1, source_target_pairs={{0,6},{2,8},{4,10},{6,12},{8,14},{10,16},{12,18},{14,20},{16,22},{... | collective-permute-start | bytes 98312 | tf_op jit(solution)/shard_map/ppermute | solution.py:18
  146.8 6.6 %collective-permute-start.1 = (f32[2,16,256]{2,1,0:T(8,128)S(1)}, f32[2,16,256]{2,1,0:T(8,128)S(1)}, u32[]{:S(2)}, u32[]{:S(2)}) collective-permute-start(f32[2,16,256]{2,1,0:T(8,128)S(1)} %get-tuple-element.10), channel_id=1, source_target_pairs={{0,4},{2,6},{4,8},{6,10},{8,12},{10,14},{12,16},{14,18},{16,20},{1... | collective-permute-start | bytes 98312 | tf_op jit(solution)/shard_map/ppermute | solution.py:18
Sparse Core Ops, SparseCore 0:
  8.9 41.7 all-gather.1
  104.8 21.5 all-reduce.1
where the time goes:
time: 161 us
  waiting for transfers between devices  63.8 us (40%)
  local copies, waits for them, and re-layouts  33 us (20%)
  matrix products  27.3 us (17%)
  between operations  14.4 us (9%)
  other arithmetic  12.4 us (8%)
  starting transfers between devices  9.98 us (6%)
    all_gather x1, waiting for transfers between devices, shards(): gathered = lax.all_gather(features, 'mp', axis=4, tiled=True)  41.4 us
    psum x1, waiting for transfers between devices, shards(): lax.psum(head_part.astype(jnp.bfloat16), 'mp').astype(jnp.float32)  16.8 us
    ppermute x8, starting transfers between devices, shifted(): return lax.ppermute(x, axis, [(i, (i + by) % count) for i in range(count)])  9.94 us
    dot_general x1, matrix products, shards(): jnp.dot(normed, w_query, preferred_element_type=jnp.float32)  5.62 us
    sub x1, other arithmetic, shards(): scores = scores - jnp.max(scores, axis=3, keepdims=True)  5.44 us
    ppermute x8, waiting for transfers between devices, shifted(): return lax.ppermute(x, axis, [(i, (i + by) % count) for i in range(count)])  4.95 us
    dot_general x1, matrix products, shards(): jnp.einsum('shqk,skhd->sqhd', attend, value_rows, preferred_element_type=...  4.91 us
    transpose x1, local copies, waits for them, and re-layouts, shards(): guided.reshape(batch_count, GRID, GRID, PATCH, PATCH, CHAN)  4.74 us
  transfers between devices with their start and end apart: 10, of which 5 were waited for; matrix products, arithmetic and copies ran while one was open for 11% of the time, Pallas kernels for 0%

commit v1 on v0

--- a/solution.py
+++ b/solution.py
@@ -60,9 +60,9 @@
     partial_value = jnp.dot(context, w_out, preferred_element_type=jnp.float32)
     head_weight = w_head.astype(jnp.float32)
     head_part = jnp.dot(partial_value, head_weight, precision=lax.Precision.HIGHEST)
-    tok_out = lax.psum(head_part.astype(jnp.bfloat16), "mp").astype(jnp.float32) + jnp.dot(
-        token_plain, w_head, preferred_element_type=jnp.float32
-    )
+    tok_out = jnp.sum(lax.all_gather(head_part.astype(jnp.bfloat16), "mp"), axis=0).astype(
+        jnp.float32
+    ) + jnp.dot(token_plain, w_head, preferred_element_type=jnp.float32)
     tok_out = tok_out.reshape(batch_count, 2, token_count, OUTW)
     guided = tok_out[:, 0] + guidance * (tok_out[:, 1] - tok_out[:, 0])
     spread = guided.reshape(batch_count, GRID, GRID, PATCH, PATCH, CHAN).transpose(0, 2, 3, 1, 4, 5)

time: 161 us -> 146 us (0.907)
  waiting for transfers between devices: 63.8 us -> 40.5 us
  blocking collectives: 0 us -> 5.73 us
  starting transfers between devices: 9.98 us -> 11.6 us
    psum x1 -> x0, waiting for transfers between devices: 16.8 us -> none  [shards(): lax.psum(head_part.astype(jnp.bfloat16), 'mp').astype(jnp.float32)]
    all_gather x1, waiting for transfers between devices: 41.4 us -> 34.8 us  [shards(): gathered = lax.all_gather(features, 'mp', axis=4, tiled=True)]
    all_gather x0 -> x1, blocking collectives: none -> 5.73 us  [shards(): lax.all_gather(head_part.astype(jnp.bfloat16), 'mp')]
    ppermute x8, starting transfers between devices: 9.94 us -> 11.6 us  [shifted(): return lax.ppermute(x, axis, [(i, (i + by) % count) for i in range(count)])]
  transfers between devices with their start and end apart: 10 -> 9, of which waited for: 5 -> 4; matrix products, arithmetic and copies ran while one was open for 11% -> 49% of each run, Pallas kernels for 0% -> 0%
where the time goes in v1:
time: 146 us; the launch traced here: 145 us
  waiting for transfers between devices  40.5 us (28%)
  local copies, waits for them, and re-layouts  33.2 us (23%)
  matrix products  26.6 us (18%)
  between operations  14.4 us (10%)
  other arithmetic  13.1 us (9%)
  starting transfers between devices  11.6 us (8%)
  blocking collectives  5.73 us (4%)
    all_gather x1, waiting for transfers between devices, shards(): gathered = lax.all_gather(features, 'mp', axis=4, tiled=True)  34.8 us
    ppermute x8, starting transfers between devices, shifted(): return lax.ppermute(x, axis, [(i, (i + by) % count) for i in range(count)])  11.6 us
    all_gather x1, blocking collectives, shards(): lax.all_gather(head_part.astype(jnp.bfloat16), 'mp')  5.73 us
    dot_general x1, matrix products, shards(): jnp.dot(normed, w_query, preferred_element_type=jnp.float32)  5.63 us
    sub x1, other arithmetic, shards(): scores = scores - jnp.max(scores, axis=3, keepdims=True)  5.43 us
    ppermute x8, waiting for transfers between devices, shifted(): return lax.ppermute(x, axis, [(i, (i + by) % count) for i in range(count)])  4.96 us
    dot_general x1, matrix products, shards(): jnp.einsum('shqk,skhd->sqhd', attend, value_rows, preferred_element_type=...  4.91 us
    transpose x1, local copies, waits for them, and re-layouts, shards(): guided.reshape(batch_count, GRID, GRID, PATCH, PATCH, CHAN)  4.52 us
  transfers between devices with their start and end apart: 9, of which 4 were waited for; matrix products, arithmetic and copies ran while one was open for 49% of the time, Pallas kernels for 0%

profile of v1, /device:TPU:0, one launch (start us, length us, event | category | flops | bytes accessed | tf_op | source)
XLA Modules:
  0.0 145.1 jit_solution(3996643897503651142)
XLA Ops:
  6.5 0.7 all-gather.3.cloned.1.call-update
  7.9 0.8 convert_bitcast_fusion
  8.7 0.1 copy.44
  8.8 0.4 dynamic_update_slice.7
  9.2 0.1 fusion.22
  9.3 0.1 copy.59
  9.4 2.4 %collective-permute-start.6 = (f32[16,64]{1,0:T(8,128)S(1)}, f32[16,64]{1,0:T(8,128)S(1)}, u32[]{:S(2)}, u32[]{:S(2)}) collective-permute-start(f32[16,64]{1,0:T(8,128)S(1)} %copy.59), channel_id=1, source_target_pairs={{0,6},{2,8},{4,10},{6,12},{8,14},{10,16},{12,18},{14,20},{16,22},{... | collective-permute-start | bytes 12296 | tf_op jit(solution)/shard_map/ppermute | solution.py:18
  11.8 0.1 copy.57
  11.9 0.8 collective-permute-start.4
  12.6 0.1 copy.58
  12.7 1.5 %collective-permute-start.5 = (f32[16,64]{1,0:T(8,128)S(1)}, f32[16,64]{1,0:T(8,128)S(1)}, u32[]{:S(2)}, u32[]{:S(2)}) collective-permute-start(f32[16,64]{1,0:T(8,128)S(1)} %copy.58), channel_id=1, source_target_pairs={{0,4},{2,6},{4,8},{6,10},{8,12},{10,14},{12,16},{14,18},{16,20},{1... | collective-permute-start | bytes 12296 | tf_op jit(solution)/shard_map/ppermute | solution.py:18
  14.2 1.6 %collective-permute-start.7 = (f32[16,64]{0,1:T(8,128)S(1)}, f32[16,64]{0,1:T(8,128)S(1)}, u32[]{:S(2)}, u32[]{:S(2)}) collective-permute-start(f32[16,64]{0,1:T(8,128)S(1)} %get-tuple-element.11), channel_id=1, source_target_pairs={{0,8},{2,10},{4,12},{6,14},{8,16},{10,18},{12,20},{14,22},{16,24},... | collective-permute-start | bytes 12296 | tf_op jit(solution)/shard_map/ppermute | solution.py:18
  15.8 0.1 copy.56
  15.8 34.8 %all-gather.3.cloned.1.call-done = bf16[1,2,2,256,1280]{4,3,2,1,0:T(8,128)(2,1)} async-done(((bf16[1,2,2,256,640]{4,3,2,1,0:T(8,128)(2,1)}), bf16[1,2,2,256,1280]{4,3,2,1,0:T(8,128)(2,1)}) %all-gather.3.cloned.1.call-update) | async-done | bytes 2621456 | tf_op jit(solution)/shard_map/all_gather | solution.py:22
  50.6 2.3 %convert_reduce_fusion = f32[2,2,256]{2,1,0:T(2,128)S(1)} fusion(bf16[1,2,2,256,1280]{4,3,2,1,0:T(8,128)(2,1)} %all-gather.3.cloned.1.call-done), kind=kLoop, calls=%fused_computation.6 | loop fusion | flops 2620416 | bytes 2625536 | tf_op jit(solution)/shard_map/reduce_sum | solution.py:30
  53.0 0.2 copy-done.1
  53.2 0.8 fusion.5
  54.0 0.0 copy-start.6
  54.0 0.7 multiply_convert_fusion
  54.7 1.5 %copy-done.2 = bf16[1024,1280]{1,0:T(8,128)(2,1)} copy-done((bf16[1024,1280]{1,0:T(8,128)(2,1)}, bf16[1024,1280]{1,0:T(8,128)(2,1)S(1)}, u32[]{:S(2)}) %copy-start.2) | copy-done | bytes 2621464
  56.2 2.2 %convolution_convert_fusion = bf16[1024,640]{1,0:T(8,128)(2,1)S(1)} fusion(bf16[1024,1280]{1,0:T(8,128)(2,1)S(1)} %multiply_convert_fusion, bf16[1280,640]{1,0:T(8,128)(2,1)S(1)} %copy-done.6), kind=kOutput, calls=%fused_computation.13 | convolution fusion | flops 1678376960 | bytes 5570560 | tf_op jit(solution)/shard_map/dot_general | solution.py:40
  58.5 1.7 %copy.35 = bf16[1024,640]{0,1:T(8,128)(2,1)} copy(bf16[1024,640]{1,0:T(8,128)(2,1)S(1)} %convolution_convert_fusion) | data formatting | bytes 2621440 | tf_op jit(solution)/shard_map/convert_element_type | solution.py:41
  60.1 2.9 %reshape.66 = bf16[4,256,10,64]{1,0,3,2:T(4,128)(2,1)S(1)} reshape(bf16[1024,640]{0,1:T(8,128)(2,1)} %copy.35) | data formatting | bytes 2621440 | tf_op jit(solution)/shard_map/reshape | solution.py:42
  63.0 0.0 copy-start.7
  63.1 5.6 %convolution_convert_fusion.1 = bf16[1024,640]{1,0:T(8,128)(2,1)} fusion(bf16[1024,1280]{1,0:T(8,128)(2,1)} %copy-done.2, bf16[1280,640]{1,0:T(8,128)(2,1)} %param.9), kind=kOutput, calls=%fused_computation.14 | convolution fusion | flops 1678376960 | bytes 5570560 | tf_op jit(solution)/shard_map/dot_general | solution.py:35
  68.7 3.3 %convolution_convert_fusion.2 = bf16[1024,640]{1,0:T(8,128)(2,1)} fusion(bf16[1024,1280]{1,0:T(8,128)(2,1)S(1)} %copy-done.3, bf16[1280,640]{1,0:T(8,128)(2,1)S(1)} %copy-done.7), kind=kOutput, calls=%fused_computation.15 | convolution fusion | flops 1678376960 | bytes 5570560 | tf_op jit(solution)/shard_map/dot_general | solution.py:45
  72.0 2.5 %copy.33 = bf16[1024,640]{0,1:T(8,128)(2,1)} copy(bf16[1024,640]{1,0:T(8,128)(2,1)} %convolution_convert_fusion.2) | data formatting | bytes 2621440 | tf_op jit(solution)/shard_map/convert_element_type | solution.py:46
  74.4 3.8 %reshape.64 = bf16[4,256,10,64]{1,0,3,2:T(4,128)(2,1)} reshape(bf16[1024,640]{0,1:T(8,128)(2,1)} %copy.33) | data formatting | bytes 2621440 | tf_op jit(solution)/shard_map/reshape | solution.py:47
  78.2 2.5 %copy.34 = bf16[1024,640]{0,1:T(8,128)(2,1)} copy(bf16[1024,640]{1,0:T(8,128)(2,1)} %convolution_convert_fusion.1) | data formatting | bytes 2621440 | tf_op jit(solution)/shard_map/convert_element_type | solution.py:36
  80.7 3.8 %reshape.65 = bf16[4,256,10,64]{1,0,3,2:T(4,128)(2,1)} reshape(bf16[1024,640]{0,1:T(8,128)(2,1)} %copy.34) | data formatting | bytes 2621440 | tf_op jit(solution)/shard_map/reshape | solution.py:37
  84.5 2.9 %fusion.11 = f32[4,10,256,256]{2,3,1,0:T(8,128)S(1)} fusion(bf16[4,256,10,64]{1,0,3,2:T(4,128)(2,1)S(1)} %reshape.66, bf16[4,256,10,64]{1,0,3,2:T(4,128)(2,1)} %reshape.65), kind=kOutput, calls=%fused_computation.18 | convolution fusion | flops 335544320 | bytes 13107200 | tf_op jit(solution)/shard_map/sqhd,skhd->shqk/dot_general | solution.py:50
  87.3 5.4 %fusion.23 = (f32[4,10,256]{2,1,0:T(8,128)S(1)}, f32[4,10,256,256]{2,3,1,0:T(8,128)}) fusion(f32[4,10,256,256]{2,3,1,0:T(8,128)S(1)} %fusion.11), kind=kOutput, calls=%fused_computation.39 | output fusion | flops 10486015 | bytes 21012480 | tf_op jit(solution)/shard_map/sub | solution.py:53
  92.8 4.9 %fusion.9 = bf16[4,256,10,64]{1,3,2,0:T(8,128)(2,1)S(1)} fusion(f32[4,10,256,256]{2,3,1,0:T(8,128)} %get-tuple-element.19, f32[4,10,256]{2,1,0:T(8,128)S(1)} %get-tuple-element.18, bf16[4,256,10,64]{1,0,3,2:T(4,128)(2,1)S(1)} %copy-done.4), kind=kOutput, calls=%fused_computation.16 | convolution fusion | flops 341442560 | bytes 13148160 | tf_op jit(solution)/shard_map/shqk,skhd->sqhd/dot_general | solution.py:56
  97.7 1.0 copy.40
  98.7 0.3 copy.62
  99.0 0.0 copy-start.5
  99.0 2.3 %fusion.24 = f32[1024,1280]{1,0:T(8,128)S(1)} fusion(bf16[1024,640]{0,1:T(8,128)(2,1)S(1)} %bitcast.59, bf16[640,1280]{1,0:T(8,128)(2,1)S(1)} %copy-done), kind=kOutput, calls=%fused_computation.40 | convolution fusion | flops 1677721600 | bytes 8192000 | tf_op jit(solution)/shard_map/dot_general | solution.py:60
  101.3 2.8 %convolution_convert_fusion.3 = bf16[1024,64]{0,1:T(8,128)(2,1)S(1)} fusion(f32[1024,1280]{1,0:T(8,128)S(1)} %fusion.24, bf16[1280,64]{0,1:T(8,128)(2,1)S(1)} %copy-done.5), kind=kOutput, calls=%fused_computation.22 | convolution fusion | flops 1006698496 | bytes 5537792 | tf_op jit(solution)/shard_map/dot_general | solution.py:62
  104.2 5.7 %all-gather = bf16[2048,64]{0,1:T(8,128)(2,1)S(1)} all-gather(bf16[1024,64]{0,1:T(8,128)(2,1)S(1)} %convolution_convert_fusion.3), channel_id=2, replica_groups=mesh['blk'=16,'mp'=2] {'mp'}, dimensions={0}, use_global_device_ids=true | all-gather | bytes 393216 | tf_op jit(solution)/shard_map/all_gather | solution.py:63
  109.9 0.2 reshape.70
  110.1 0.7 reduce_sum.42
  110.8 2.6 %convolution_add_fusion = f32[1024,64]{0,1:T(8,128)S(1)} fusion(bf16[1024,1280]{1,0:T(8,128)(2,1)} %bitcast.57, bf16[1280,64]{0,1:T(8,128)(2,1)S(1)} %copy-done.5, bf16[1024,64]{0,1:T(8,128)(2,1)S(1)} %reduce_sum.42), kind=kOutput, calls=%fused_computation.21 | convolution fusion | flops 167903232 | bytes 3178496 | tf_op jit(solution)/shard_map/dot_general | solution.py:65
  113.4 0.2 reshape.68
  113.6 0.2 fusion.20
  113.9 1.3 squeeze.11
  115.2 1.3 squeeze.12
  116.5 1.7 %add_bitcast_fusion = f32[2,16,4,16,4,4]{1,3,5,4,2,0:T(8,128)S(1)} fusion(f32[2,16,16,4,4,4]{2,1,5,4,3,0:T(8,128)} %squeeze.11, f32[2,16,16,4,4,4]{2,1,5,4,3,0:T(8,128)} %squeeze.12), kind=kLoop, calls=%fused_computation.23 | loop fusion | flops 98304 | bytes 393216 | tf_op jit(solution)/shard_map/transpose | solution.py:68
  118.2 4.5 %copy.43 = f32[2,16,4,16,4,4]{2,1,5,4,3,0:T(8,128)} copy(f32[2,16,4,16,4,4]{1,3,5,4,2,0:T(8,128)S(1)} %add_bitcast_fusion) | data formatting | bytes 262144 | tf_op jit(solution)/shard_map/transpose | solution.py:68
  122.8 3.6 %reshape.69 = f32[2,64,256]{1,2,0:T(8,128)S(1)} reshape(f32[2,16,4,16,4,4]{2,1,5,4,3,0:T(8,128)} %copy.43) | data formatting | bytes 262144 | tf_op jit(solution)/shard_map/reshape | solution.py:69
  126.5 0.1 copy.45
  126.6 0.4 dynamic_update_slice.6
  127.1 0.1 collective-permute-start
  127.1 0.0 collective-permute-done.6
  127.1 1.5 %collective-permute-start.3 = (f32[2,16,256]{2,1,0:T(8,128)S(1)}, f32[2,16,256]{2,1,0:T(8,128)S(1)}, u32[]{:S(2)}, u32[]{:S(2)}) collective-permute-start(f32[2,16,256]{2,1,0:T(8,128)S(1)} %get-tuple-element.8), channel_id=1, source_target_pairs={{0,8},{2,10},{4,12},{6,14},{8,16},{10,18},{12,20},{14,22},{16,24},... | collective-permute-start | bytes 98312 | tf_op jit(solution)/shard_map/ppermute | solution.py:18
  128.7 2.3 %collective-permute-start.2 = (f32[2,16,256]{2,1,0:T(8,128)S(1)}, f32[2,16,256]{2,1,0:T(8,128)S(1)}, u32[]{:S(2)}, u32[]{:S(2)}) collective-permute-start(f32[2,16,256]{2,1,0:T(8,128)S(1)} %get-tuple-element.9), channel_id=1, source_target_pairs={{0,6},{2,8},{4,10},{6,12},{8,14},{10,16},{12,18},{14,20},{16,22},{... | collective-permute-start | bytes 98312 | tf_op jit(solution)/shard_map/ppermute | solution.py:18
  131.0 0.0 collective-permute-done.5
  131.0 1.5 %collective-permute-start.1 = (f32[2,16,256]{2,1,0:T(8,128)S(1)}, f32[2,16,256]{2,1,0:T(8,128)S(1)}, u32[]{:S(2)}, u32[]{:S(2)}) collective-permute-start(f32[2,16,256]{2,1,0:T(8,128)S(1)} %get-tuple-element.10), channel_id=1, source_target_pairs={{0,4},{2,6},{4,8},{6,10},{8,12},{10,14},{12,16},{14,18},{16,20},{1... | collective-permute-start | bytes 98312 | tf_op jit(solution)/shard_map/ppermute | solution.py:18
  132.5 0.1 copy.51
  132.6 0.0 collective-permute-done.7
  132.6 0.1 copy.52
  132.7 0.5 collective-permute-done
  133.2 0.7 collective-permute-done.2
  133.8 3.8 %collective-permute-done.1 = f32[2,16,256]{2,1,0:T(8,128)S(1)} collective-permute-done((f32[2,16,256]{2,1,0:T(8,128)S(1)}, f32[2,16,256]{2,1,0:T(8,128)S(1)}, u32[]{:S(2)}, u32[]{:S(2)}) %collective-permute-start.1) | collective-permute-done | bytes 32800 | tf_op jit(solution)/shard_map/ppermute | solution.py:18
  137.6 0.6 fusion.17
  (28 shorter events, 0.2 us)
Async XLA Ops:
  6.5 92.5 %copy-start = (bf16[640,1280]{1,0:T(8,128)(2,1)S(1)}, bf16[640,1280]{1,0:T(8,128)(2,1)}, u32[]{:S(2)}) copy-start(bf16[640,1280]{1,0:T(8,128)(2,1)} %param.12) | copy-start | bytes 4915204
  6.5 44.1 %all-gather.3.cloned.1.call-start = ((), (), s32[]{:S(2)}) async-start(), calls=%async_computation | async-start | bytes 3932160 | tf_op jit(solution)/shard_map/all_gather | solution.py:22
  9.4 117.8 %collective-permute-start.6 = (f32[16,64]{1,0:T(8,128)S(1)}, f32[16,64]{1,0:T(8,128)S(1)}, u32[]{:S(2)}, u32[]{:S(2)}) collective-permute-start(f32[16,64]{1,0:T(8,128)S(1)} %copy.59), channel_id=1, source_target_pairs={{0,6},{2,8},{4,10},{6,12},{8,14},{10,16},{12,18},{14,20},{16,22},{... | collective-permute-start | bytes 12296 | tf_op jit(solution)/shard_map/ppermute | solution.py:18
  11.9 116.8 %collective-permute-start.4 = (f32[16,64]{1,0:T(8,128)S(1)}, f32[16,64]{1,0:T(8,128)S(1)}, u32[]{:S(2)}, u32[]{:S(2)}) collective-permute-start(f32[16,64]{1,0:T(8,128)S(1)} %copy.57), channel_id=1, source_target_pairs={{0,2},{2,4},{4,6},{6,8},{8,10},{10,12},{12,14},{14,16},{16,18},{18... | collective-permute-start | bytes 12296 | tf_op jit(solution)/shard_map/ppermute | solution.py:18
  12.7 118.3 %collective-permute-start.5 = (f32[16,64]{1,0:T(8,128)S(1)}, f32[16,64]{1,0:T(8,128)S(1)}, u32[]{:S(2)}, u32[]{:S(2)}) collective-permute-start(f32[16,64]{1,0:T(8,128)S(1)} %copy.58), channel_id=1, source_target_pairs={{0,4},{2,6},{4,8},{6,10},{8,12},{10,14},{12,16},{14,18},{16,20},{1... | collective-permute-start | bytes 12296 | tf_op jit(solution)/shard_map/ppermute | solution.py:18
  14.2 118.4 %collective-permute-start.7 = (f32[16,64]{0,1:T(8,128)S(1)}, f32[16,64]{0,1:T(8,128)S(1)}, u32[]{:S(2)}, u32[]{:S(2)}) collective-permute-start(f32[16,64]{0,1:T(8,128)S(1)} %get-tuple-element.11), channel_id=1, source_target_pairs={{0,8},{2,10},{4,12},{6,14},{8,16},{10,18},{12,20},{14,22},{16,24},... | collective-permute-start | bytes 12296 | tf_op jit(solution)/shard_map/ppermute | solution.py:18
  50.6 2.5 %copy-start.1 = (bf16[1,2,2,256,1280]{4,3,2,1,0:T(8,128)(2,1)S(1)}, bf16[1,2,2,256,1280]{4,3,2,1,0:T(8,128)(2,1)}, u32[]{:S(2)}) copy-start(bf16[1,2,2,256,1280]{4,3,2,1,0:T(8,128)(2,1)} %all-gather.3.cloned.1.call-done) | copy-start | bytes 7864324
  54.0 2.2 %copy-start.6 = (bf16[1280,640]{1,0:T(8,128)(2,1)S(1)}, bf16[1280,640]{1,0:T(8,128)(2,1)}, u32[]{:S(2)}) copy-start(bf16[1280,640]{1,0:T(8,128)(2,1)} %param.10) | copy-start | bytes 4915204
  54.7 1.5 %copy-start.2 = (bf16[1024,1280]{1,0:T(8,128)(2,1)}, bf16[1024,1280]{1,0:T(8,128)(2,1)S(1)}, u32[]{:S(2)}) copy-start(bf16[1024,1280]{1,0:T(8,128)(2,1)S(1)} %multiply_convert_fusion) | copy-start | bytes 7864324
  63.0 5.7 %copy-start.3 = (bf16[1024,1280]{1,0:T(8,128)(2,1)S(1)}, bf16[1024,1280]{1,0:T(8,128)(2,1)}, u32[]{:S(2)}) copy-start(bf16[1024,1280]{1,0:T(8,128)(2,1)} %copy-done.2) | copy-start | bytes 7864324
  63.0 5.6 %copy-start.7 = (bf16[1280,640]{1,0:T(8,128)(2,1)S(1)}, bf16[1280,640]{1,0:T(8,128)(2,1)}, u32[]{:S(2)}) copy-start(bf16[1280,640]{1,0:T(8,128)(2,1)} %param.11) | copy-start | bytes 4915204
  87.3 5.4 %copy-start.4 = (bf16[4,256,10,64]{1,0,3,2:T(4,128)(2,1)S(1)}, bf16[4,256,10,64]{1,0,3,2:T(4,128)(2,1)}, u32[]{:S(2)}) copy-start(bf16[4,256,10,64]{1,0,3,2:T(4,128)(2,1)} %reshape.64) | copy-start | bytes 3932164
  99.0 2.3 %copy-start.5 = (bf16[1280,64]{0,1:T(8,128)(2,1)S(1)}, bf16[1280,64]{0,1:T(8,128)(2,1)}, u32[]{:S(2)}) copy-start(bf16[1280,64]{0,1:T(8,128)(2,1)} %param.13) | copy-start | bytes 491524
  127.1 6.1 %collective-permute-start = (f32[2,16,256]{2,1,0:T(8,128)S(1)}, f32[2,16,256]{2,1,0:T(8,128)S(1)}, u32[]{:S(2)}, u32[]{:S(2)}) collective-permute-start(f32[2,16,256]{2,1,0:T(8,128)S(1)} %get-tuple-element.7), channel_id=1, source_target_pairs={{0,2},{2,4},{4,6},{6,8},{8,10},{10,12},{12,14},{14,16},{16,18},{18... | collective-permute-start | bytes 98312 | tf_op jit(solution)/shard_map/ppermute | solution.py:18
  127.1 6.0 %collective-permute-start.3 = (f32[2,16,256]{2,1,0:T(8,128)S(1)}, f32[2,16,256]{2,1,0:T(8,128)S(1)}, u32[]{:S(2)}, u32[]{:S(2)}) collective-permute-start(f32[2,16,256]{2,1,0:T(8,128)S(1)} %get-tuple-element.8), channel_id=1, source_target_pairs={{0,8},{2,10},{4,12},{6,14},{8,16},{10,18},{12,20},{14,22},{16,24},... | collective-permute-start | bytes 98312 | tf_op jit(solution)/shard_map/ppermute | solution.py:18
  128.7 5.1 %collective-permute-start.2 = (f32[2,16,256]{2,1,0:T(8,128)S(1)}, f32[2,16,256]{2,1,0:T(8,128)S(1)}, u32[]{:S(2)}, u32[]{:S(2)}) collective-permute-start(f32[2,16,256]{2,1,0:T(8,128)S(1)} %get-tuple-element.9), channel_id=1, source_target_pairs={{0,6},{2,8},{4,10},{6,12},{8,14},{10,16},{12,18},{14,20},{16,22},{... | collective-permute-start | bytes 98312 | tf_op jit(solution)/shard_map/ppermute | solution.py:18
  131.0 6.6 %collective-permute-start.1 = (f32[2,16,256]{2,1,0:T(8,128)S(1)}, f32[2,16,256]{2,1,0:T(8,128)S(1)}, u32[]{:S(2)}, u32[]{:S(2)}) collective-permute-start(f32[2,16,256]{2,1,0:T(8,128)S(1)} %get-tuple-element.10), channel_id=1, source_target_pairs={{0,4},{2,6},{4,8},{6,10},{8,12},{10,14},{12,16},{14,18},{16,20},{1... | collective-permute-start | bytes 98312 | tf_op jit(solution)/shard_map/ppermute | solution.py:18
Sparse Core Ops, SparseCore 0:
  8.9 41.7 all-gather.2
